TPU v7x, 32 devices: a whole 2x2x4 slice. The times are simulated.
32 devices in a mesh: dp: 4 (over y, x), mp: 8 (over z, core).
Axes of the slice: x: 2, y: 2, z: 4, core: 2. Of those that a mesh axis runs over, the one named last changes fastest.
Arguments:
- tokens: bfloat16 [512, 6144], P(('dp', 'mp')), may hold values from -6 to 6
- norm_gain: float32 [6144], replicated, may hold values from 0.5 to 1.5
- up_weight: bfloat16 [6144, 16384], P(None, 'mp'), may hold values from -0.078125 to 0.078125
- down_weight: bfloat16 [16384, 6144], P('mp'), may hold values from -0.046875 to 0.046875
- out_grad: bfloat16 [512, 6144], P(('dp', 'mp')), may hold values from -6 to 6
Outputs:
- input_grad: bfloat16 [512, 6144], P(('dp', 'mp'))
- up_grad: bfloat16 [6144, 16384], P('dp', 'mp')
- down_grad: bfloat16 [16384, 6144], P('mp', 'dp')
- gain_grad: float32 [6144], replicated
All inputs are finite; a program needn't handle non-finite values.
Results may differ from a plain program's by a relative error of at most 0.018.
Values may be sent and summed in bfloat16 or wider, within the bound.
No kernel may reach another device: no remote copies, remote signals or barrier semaphores. Data moves between devices by JAX's collectives and lax.ppermute only.
A program may use at most 192 MiB of HBM per device.

v0:
```python
import math
import jax
import jax.numpy as jnp
from jax import lax
from jax.sharding import PartitionSpec as P


def gelu_value(preact):
    return 0.5 * preact * (1.0 + lax.erf(preact * 0.7071067811865476))


def gelu_slope(preact):
    return (
        0.5 * (1.0 + lax.erf(preact * 0.7071067811865476))
        + preact * jnp.exp(-0.5 * preact * preact) * 0.3989422804014327
    )


def per_device(tokens, norm_gain, up_weight, down_weight, out_grad):
    values = tokens.astype(jnp.float32)
    centered = values - jnp.mean(values, axis=1, keepdims=True)
    inv_std = lax.rsqrt(jnp.mean(centered * centered, axis=1, keepdims=True) + 1e-06)
    x_hat = centered * inv_std
    normed = (x_hat * norm_gain).astype(jnp.bfloat16)
    normed_all, cotan_all = (
        lax.all_gather(normed, "mp", axis=0, tiled=True),
        lax.all_gather(out_grad, "mp", axis=0, tiled=True),
    )
    preact = jnp.dot(normed_all, up_weight, preferred_element_type=jnp.float32)
    hidden = gelu_value(preact).astype(jnp.bfloat16)
    hid_grad = lax.dot_general(
        cotan_all, down_weight, (((1,), (1,)), ((), ())), preferred_element_type=jnp.float32
    )
    pre_grad = (hid_grad * gelu_slope(preact)).astype(jnp.bfloat16)
    norm_grad = lax.psum_scatter(
        lax.dot_general(
            pre_grad, up_weight, (((1,), (1,)), ((), ())), preferred_element_type=jnp.float32
        ),
        "mp",
        scatter_dimension=0,
        tiled=True,
    )
    replicas = lax.axis_size("dp")
    group = normed_all.shape[0]
    factor = 1.0 / math.sqrt(group * replicas)
    gain_grad = lax.psum(jnp.sum(norm_grad * x_hat, axis=0), ("dp", "mp")) * factor
    scaled = norm_gain * norm_grad
    input_grad = (
        scaled
        - jnp.mean(scaled, axis=1, keepdims=True)
        - x_hat * jnp.mean(scaled * x_hat, axis=1, keepdims=True)
    ) * inv_std
    normed_cols, cotan_cols = (
        lax.all_to_all(normed_all, "dp", split_axis=1, concat_axis=0, tiled=True),
        lax.all_to_all(cotan_all, "dp", split_axis=1, concat_axis=0, tiled=True),
    )
    hidden_all, pre_all = (
        lax.all_gather(hidden, "dp", axis=0, tiled=True),
        lax.all_gather(pre_grad, "dp", axis=0, tiled=True),
    )

    def stacked(array):
        return array.reshape(replicas, group, array.shape[1])

    up_parts = jnp.einsum(
        "rtk,rtf->rkf", stacked(normed_cols), stacked(pre_all), preferred_element_type=jnp.float32
    )
    down_parts = jnp.einsum(
        "rtf,rtk->rfk", stacked(hidden_all), stacked(cotan_cols), preferred_element_type=jnp.float32
    )
    up_total = jnp.sum(up_parts.astype(jnp.bfloat16).astype(jnp.float32), axis=0)
    down_total = jnp.sum(down_parts.astype(jnp.bfloat16).astype(jnp.float32), axis=0)
    up_grad = (up_total * factor).astype(jnp.bfloat16)
    down_grad = (down_total * factor).astype(jnp.bfloat16)
    return (input_grad.astype(jnp.bfloat16), up_grad, down_grad, gain_grad)


def solution(mesh):
    placed = (P(("dp", "mp"), None), P(), P(None, "mp"), P("mp", None), P(("dp", "mp"), None))
    return jax.shard_map(
        per_device,
        mesh=mesh,
        in_specs=placed,
        out_specs=(P(("dp", "mp"), None), P("dp", "mp"), P("mp", "dp"), P()),
        check_vma=False,
    )
```

profile of v0, /device:TPU:10, one launch (start us, length us, event | category | flops | bytes accessed | tf_op | source)
XLA Modules:
  0.0 251.2 jit_solution(14012743861452806159)
XLA Ops:
  7.2 0.0 all-gather.7.cloned.1.call-start
  7.2 1.1 convert_reduce_fusion.2
  8.3 1.2 fusion.19
  9.5 1.7 fusion.13
  11.2 0.0 all-gather.7.cloned.1.call-update
  11.2 0.0 all-gather.5.cloned.1.call-start
  11.3 0.7 all-gather.5.cloned.1.call-update
  12.0 0.0 all-gather.11.cloned.1.call-start
  12.0 25.4 %all-gather.7.cloned.1.call-done = bf16[128,6144]{1,0:T(8,128)(2,1)} async-done(((bf16[16,6144]{1,0:T(8,128)(2,1)}), bf16[128,6144]{1,0:T(8,128)(2,1)}) %all-gather.7.cloned.1.call-update) | async-done | bytes 1572880 | tf_op jit(solution)/shard_map/all_gather | solution.py:26
  37.5 13.1 %multiply_convert_fusion.2 = (bf16[128,2048]{1,0:T(8,128)(2,1)}, f32[128,2048]{1,0:T(8,128)S(1)}) fusion(bf16[128,6144]{1,0:T(8,128)(2,1)} %all-gather.7.cloned.1.call-done, bf16[6144,2048]{1,0:T(8,128)(2,1)} %param.7), kind=kOutput, calls=%fused_computation.15 | convolution fusion | flops 3222536192 | bytes 28311552 | tf_op jit(solution)/shard_map/dot_general | solution.py:29
  50.6 0.0 all-gather.11.cloned.1.call-update
  50.6 0.0 all-gather.9.cloned.1.call-start
  50.6 12.9 %all-gather.5.cloned.1.call-done = bf16[128,6144]{1,0:T(8,128)(2,1)} async-done(((bf16[16,6144]{1,0:T(8,128)(2,1)}), bf16[128,6144]{1,0:T(8,128)(2,1)}) %all-gather.5.cloned.1.call-update) | async-done | bytes 1572880 | tf_op jit(solution)/shard_map/all_gather | solution.py:27
  63.5 14.3 %fusion = bf16[128,2048]{1,0:T(8,128)(2,1)} fusion(bf16[128,6144]{1,0:T(8,128)(2,1)} %all-gather.5.cloned.1.call-done, bf16[2048,6144]{1,0:T(8,128)(2,1)} %param.8, f32[128,2048]{1,0:T(8,128)S(1)} %get-tuple-element.8), kind=kOutput, calls=%fused_computation.7 | convolution fusion | flops 3223846912 | bytes 28311552 | tf_op jit(solution)/shard_map/dot_general | solution.py:31
  77.8 0.0 all-gather.9.cloned.1.call-update
  77.8 0.0 copy-start
  77.9 0.0 reduce-scatter.2.cloned.1.call-start
  77.9 14.4 %fusion.20 = f32[128,6144]{1,0:T(8,128)} fusion(bf16[128,2048]{1,0:T(8,128)(2,1)} %fusion, bf16[6144,2048]{1,0:T(8,128)(2,1)} %param.7), kind=kOutput, calls=%fused_computation.38 | convolution fusion | flops 3221225472 | bytes 28835840 | tf_op jit(solution)/shard_map/dot_general | solution.py:36
  92.4 0.0 copy-start.1
  92.4 0.0 reduce-scatter.2.cloned.1.call-update
  92.4 0.0 copy-done
  92.4 1.6 copy.16
  94.0 2.6 %copy.17 = bf16[128,4,1536]{2,0,1:T(8,128)(2,1)} copy(bf16[128,4,1536]{0,2,1:T(8,128)(2,1)} %bitcast.18) | data formatting | bytes 3145728 | tf_op jit(solution)/shard_map/all_to_all | solution.py:55
  96.5 4.2 %all-to-all-start.1 = ((bf16[128,4,1536]{2,0,1:T(8,128)(2,1)}), bf16[128,4,1536]{2,0,1:T(8,128)(2,1)S(1)}, u32[]{:S(2)}, u32[]{:S(2)}) async-start(bf16[128,4,1536]{2,0,1:T(8,128)(2,1)} %copy.17), calls=%async_computation.2 | async-start | bytes 3145728 | tf_op jit(solution)/shard_map/all_to_all | solution.py:55
  100.7 0.0 copy-done.1
  100.7 1.6 copy.20
  102.3 23.3 %all-to-all-done.1 = bf16[128,4,1536]{2,0,1:T(8,128)(2,1)S(1)} async-done(((bf16[128,4,1536]{2,0,1:T(8,128)(2,1)}), bf16[128,4,1536]{2,0,1:T(8,128)(2,1)S(1)}, u32[]{:S(2)}, u32[]{:S(2)}) %all-to-all-start.1) | async-done | bytes 1572896 | tf_op jit(solution)/shard_map/all_to_all | solution.py:55
  125.6 4.1 %all-to-all-start = ((bf16[128,4,1536]{0,2,1:T(8,128)(2,1)}), bf16[128,4,1536]{0,2,1:T(8,128)(2,1)S(1)}, u32[]{:S(2)}, u32[]{:S(2)}) async-start(bf16[128,4,1536]{0,2,1:T(8,128)(2,1)} %bitcast), calls=%async_computation.1 | async-start | bytes 3145728 | tf_op jit(solution)/shard_map/all_to_all | solution.py:54
  129.7 0.0 all-gather.11.cloned.1.call-done
  129.7 14.2 %convert_reduce_fusion = f32[2048,1536]{1,0:T(8,128)} fusion(bf16[4,128,2048]{2,1,0:T(8,128)(2,1)} %bitcast.19, bf16[128,4,1536]{2,0,1:T(8,128)(2,1)S(1)} %all-to-all-done.1), kind=kOutput, calls=%fused_computation | convolution fusion | flops 3255828480 | bytes 16252928 | tf_op jit(solution)/shard_map/rtf,rtk->rfk/dot_general | solution.py:68
  143.9 15.4 %all-to-all-done = bf16[128,4,1536]{0,2,1:T(8,128)(2,1)S(1)} async-done(((bf16[128,4,1536]{0,2,1:T(8,128)(2,1)}), bf16[128,4,1536]{0,2,1:T(8,128)(2,1)S(1)}, u32[]{:S(2)}, u32[]{:S(2)}) %all-to-all-start) | async-done | bytes 1572896 | tf_op jit(solution)/shard_map/all_to_all | solution.py:54
  159.3 0.0 all-gather.9.cloned.1.call-done
  159.3 14.0 %convert_reduce_fusion.1 = f32[1536,2048]{1,0:T(8,128)} fusion(bf16[4,128,2048]{2,1,0:T(8,128)(2,1)} %bitcast.20, bf16[128,4,1536]{0,2,1:T(8,128)(2,1)S(1)} %all-to-all-done), kind=kOutput, calls=%fused_computation.1 | convolution fusion | flops 3255828480 | bytes 16252928 | tf_op jit(solution)/shard_map/rtk,rtf->rkf/dot_general | solution.py:65
  173.3 9.2 %multiply_convert_fusion = bf16[2048,1536]{1,0:T(8,128)(2,1)} fusion(f32[2048,1536]{1,0:T(8,128)} %convert_reduce_fusion), kind=kLoop, calls=%fused_computation.4 | loop fusion | flops 6291456 | bytes 18874368 | tf_op jit(solution)/shard_map/convert_element_type | solution.py:74
  182.4 0.0 copy-start.2
  182.4 0.0 copy-start.3
  182.4 9.3 %multiply_convert_fusion.1 = bf16[1536,2048]{1,0:T(8,128)(2,1)} fusion(f32[1536,2048]{1,0:T(8,128)} %convert_reduce_fusion.1), kind=kLoop, calls=%fused_computation.5 | loop fusion | flops 6291456 | bytes 18874368 | tf_op jit(solution)/shard_map/convert_element_type | solution.py:73
  191.7 4.7 %reduce-scatter.2.cloned.1.call-done = f32[16,6144]{1,0:T(8,128)} async-done(((f32[128,6144]{1,0:T(8,128)}), f32[16,6144]{1,0:T(8,128)}) %reduce-scatter.2.cloned.1.call-update) | async-done | bytes 393232 | tf_op jit(solution)/shard_map/reduce_scatter | solution.py:35
  196.5 0.0 copy-done.2
  196.5 0.0 copy-done.3
  196.5 1.3 fusion.18
  197.8 44.4 %psum.7 = f32[6144]{0:T(1024)S(1)} all-reduce(f32[6144]{0:T(1024)S(1)} %get-tuple-element.4), channel_id=1, replica_groups=mesh['dp'=4,'mp'=8] {'dp','mp'}, use_global_device_ids=true, to_apply=%region_8.0 | all-reduce | flops 6144 | bytes 49152 | tf_op jit(solution)/shard_map/psum | solution.py:46
  242.2 0.6 broadcast_multiply_fusion
  242.8 1.8 fusion.17
  (3 shorter events, 0.0 us)
Async XLA Ops:
  7.2 30.3 %all-gather.7.cloned.1.call-start = ((), (), s32[]{:S(2)}) async-start(), calls=%async_computation.4 | async-start | bytes 1769472 | tf_op jit(solution)/shard_map/all_gather | solution.py:26
  11.2 52.3 %all-gather.5.cloned.1.call-start = ((), (), s32[]{:S(2)}) async-start(), calls=%async_computation.3 | async-start | bytes 1769472 | tf_op jit(solution)/shard_map/all_gather | solution.py:27
  12.0 117.7 %all-gather.11.cloned.1.call-start = ((), (), s32[]{:S(2)}) async-start(), calls=%async_computation.7 | async-start | bytes 2621440 | tf_op jit(solution)/shard_map/all_gather | solution.py:58
  50.6 108.7 %all-gather.9.cloned.1.call-start = ((), (), s32[]{:S(2)}) async-start(), calls=%async_computation.6 | async-start | bytes 2621440 | tf_op jit(solution)/shard_map/all_gather | solution.py:59
  77.8 14.5 %copy-start = (bf16[128,6144]{1,0:T(8,128)(2,1)S(1)}, bf16[128,6144]{1,0:T(8,128)(2,1)}, u32[]{:S(2)}) copy-start(bf16[128,6144]{1,0:T(8,128)(2,1)} %all-gather.5.cloned.1.call-done) | copy-start | bytes 4718596
  77.9 118.6 %reduce-scatter.2.cloned.1.call-start = ((), (), s32[]{:S(2)}) async-start(), calls=%async_computation.5 | async-start | bytes 3538944 | tf_op jit(solution)/shard_map/reduce_scatter | solution.py:35
  92.4 8.4 %copy-start.1 = (bf16[128,6144]{1,0:T(8,128)(2,1)S(1)}, bf16[128,6144]{1,0:T(8,128)(2,1)}, u32[]{:S(2)}) copy-start(bf16[128,6144]{1,0:T(8,128)(2,1)} %all-gather.7.cloned.1.call-done) | copy-start | bytes 4718596
  96.5 29.0 %all-to-all-start.1 = ((bf16[128,4,1536]{2,0,1:T(8,128)(2,1)}), bf16[128,4,1536]{2,0,1:T(8,128)(2,1)S(1)}, u32[]{:S(2)}, u32[]{:S(2)}) async-start(bf16[128,4,1536]{2,0,1:T(8,128)(2,1)} %copy.17), calls=%async_computation.2 | async-start | bytes 3145728 | tf_op jit(solution)/shard_map/all_to_all | solution.py:55
  125.6 33.7 %all-to-all-start = ((bf16[128,4,1536]{0,2,1:T(8,128)(2,1)}), bf16[128,4,1536]{0,2,1:T(8,128)(2,1)S(1)}, u32[]{:S(2)}, u32[]{:S(2)}) async-start(bf16[128,4,1536]{0,2,1:T(8,128)(2,1)} %bitcast), calls=%async_computation.1 | async-start | bytes 3145728 | tf_op jit(solution)/shard_map/all_to_all | solution.py:54
  182.4 14.0 %copy-start.2 = (bf16[16,6144]{1,0:T(8,128)(2,1)S(1)}, bf16[16,6144]{1,0:T(8,128)(2,1)}, u32[]{:S(2)}) copy-start(bf16[16,6144]{1,0:T(8,128)(2,1)} %param.5) | copy-start | bytes 589828
  182.4 14.0 %copy-start.3 = (f32[6144]{0:T(1024)S(1)}, f32[6144]{0:T(1024)}, u32[]{:S(2)}) copy-start(f32[6144]{0:T(1024)} %param.6) | copy-start | bytes 73732
Sparse Core Ops, SparseCore 0:
  11.4 26.0 all-gather.6
  39.1 24.3 all-gather.4
  65.4 34.6 all-gather.10
  101.8 52.6 all-gather.8
  156.6 39.8 reduce-scatter.1
where the time goes:
time: 252 us; the launch traced here: 251 us
  waiting for transfers between devices  82.5 us (33%)
  matrix products  69.9 us (28%)
  blocking collectives  44.4 us (18%)
  other arithmetic  26.2 us (10%)
  between operations  13.8 us (5%)
  starting transfers between devices  8.55 us (3%)
  local copies, waits for them, and re-layouts  5.71 us (2%)
    psum x1, blocking collectives, per_device(): lax.psum(jnp.sum(norm_grad * x_hat, axis=0), ('dp', 'mp')) * factor  44.4 us
    all_gather x1, waiting for transfers between devices, per_device(): lax.all_gather(normed, 'mp', axis=0, tiled=True)  25.4 us
    all_to_all x1, waiting for transfers between devices, per_device(): lax.all_to_all(cotan_all, 'dp', split_axis=1, concat_axis=0, tiled=True)  23.3 us
    all_to_all x1, waiting for transfers between devices, per_device(): lax.all_to_all(normed_all, 'dp', split_axis=1, concat_axis=0, tiled=True)  15.4 us
    dot_general x1, matrix products, per_device(): lax.dot_general(pre_grad, up_weight, (((1,), (1,)), ((), ())), preferred_...  14.4 us
    dot_general x1, matrix products, per_device(): lax.dot_general(cotan_all, down_weight, (((1,), (1,)), ((), ())), preferr...  14.3 us
    dot_general x1, matrix products, per_device(): jnp.einsum('rtf,rtk->rfk', stacked(hidden_all), stacked(cotan_cols), pref...  14.2 us
    dot_general x1, matrix products, per_device(): jnp.einsum('rtk,rtf->rkf', stacked(normed_cols), stacked(pre_all), prefer...  14 us
  transfers between devices with their start and end apart: 7, of which 5 were waited for; matrix products, arithmetic and copies ran while one was open for 37% of the time, Pallas kernels for 0%

commit v1 on v0

--- a/solution.py
+++ b/solution.py
@@ -3,6 +3,27 @@
 import jax.numpy as jnp
 from jax import lax
 from jax.sharding import PartitionSpec as P
+
+
+def ring_gather(shard, axis, dim):
+    size, index, rows = (lax.axis_size(axis), lax.axis_index(axis), shard.shape[dim])
+    forward = [(i, (i + 1) % size) for i in range(size)]
+    behind = [(i, (i - 1) % size) for i in range(size)]
+    result = jnp.zeros((*shard.shape[:dim], size * rows, *shard.shape[dim + 1 :]), shard.dtype)
+    result = lax.dynamic_update_slice_in_dim(result, shard, index * rows, axis=dim)
+    from_left = from_right = shard
+    middle = size // 2
+    for lap in range(1, middle + 1):
+        from_left = lax.ppermute(from_left, axis, forward)
+        result = lax.dynamic_update_slice_in_dim(
+            result, from_left, (index - lap) % size * rows, axis=dim
+        )
+        if lap < size - middle:
+            from_right = lax.ppermute(from_right, axis, behind)
+            result = lax.dynamic_update_slice_in_dim(
+                result, from_right, (index + lap) % size * rows, axis=dim
+            )
+    return result
 
 
 def gelu_value(preact):
@@ -23,7 +44,7 @@
     x_hat = centered * inv_std
     normed = (x_hat * norm_gain).astype(jnp.bfloat16)
     normed_all, cotan_all = (
-        lax.all_gather(normed, "mp", axis=0, tiled=True),
+        ring_gather(normed, "mp", 0),
         lax.all_gather(out_grad, "mp", axis=0, tiled=True),
     )
     preact = jnp.dot(normed_all, up_weight, preferred_element_type=jnp.float32)

time: 252 us -> 380 us (1.51)
  local copies, waits for them, and re-layouts: 5.71 us -> 138 us
  waiting for transfers between devices: 82.5 us -> 44.6 us
  blocking collectives: 44.4 us -> 73.3 us
  starting transfers between devices: 8.55 us -> 12.4 us
    dynamic_update_slice x0 -> x8, local copies, waits for them, and re-layouts: none -> 127 us  [the longest x4 62.4 us: ring_gather(): lax.dynamic_update_slice_in_dim(result, from_left, (index - lap) % size *...]
    all_to_all x0 -> x1, blocking collectives: none -> 28.7 us  [per_device(): lax.all_to_all(cotan_all, 'dp', split_axis=1, concat_axis=0, tiled=True)]
    all_gather x1 -> x0, waiting for transfers between devices: 25.4 us -> none  [per_device(): lax.all_gather(normed, 'mp', axis=0, tiled=True)]
    all_to_all x1 -> x0, waiting for transfers between devices: 23.3 us -> none  [per_device(): lax.all_to_all(cotan_all, 'dp', split_axis=1, concat_axis=0, tiled=True)]
    ppermute x0 -> x7, waiting for transfers between devices: none -> 18 us  [the longest x3 13.4 us: ring_gather(): from_right = lax.ppermute(from_right, axis, behind)]
    reduce_scatter x1, waiting for transfers between devices: 4.71 us -> 18.9 us  [per_device(): lax.psum_scatter(lax.dot_general(pre_grad, up_weight, (((1,), (1,)), ((),...]
    all_gather x1, waiting for transfers between devices: 12.9 us -> 0.02 us  [per_device(): lax.all_gather(out_grad, 'mp', axis=0, tiled=True)]
    all_to_all x1, waiting for transfers between devices: 15.4 us -> 7.43 us  [per_device(): lax.all_to_all(normed_all, 'dp', split_axis=1, concat_axis=0, tiled=True)]
  transfers between devices with their start and end apart: 7 -> 12, of which waited for: 5 -> 7; matrix products, arithmetic and copies ran while one was open for 37% -> 60% of each run, Pallas kernels for 0% -> 0%
where the time goes in v1:
time: 380 us; the launch traced here: 378 us
  local copies, waits for them, and re-layouts  138 us (36%)
  blocking collectives  73.3 us (19%)
  matrix products  69.9 us (18%)
  waiting for transfers between devices  44.6 us (12%)
  other arithmetic  25.4 us (7%)
  between operations  13.9 us (4%)
  starting transfers between devices  12.4 us (3%)
    dynamic_update_slice x4, local copies, waits for them, and re-layouts, ring_gather(): lax.dynamic_update_slice_in_dim(result, from_left, (index - lap) % size *...  62.4 us
    dynamic_update_slice x3, local copies, waits for them, and re-layouts, ring_gather(): lax.dynamic_update_slice_in_dim(result, from_right, (index + lap) % size...  48.7 us
    psum x1, blocking collectives, per_device(): lax.psum(jnp.sum(norm_grad * x_hat, axis=0), ('dp', 'mp')) * factor  44.6 us
    all_to_all x1, blocking collectives, per_device(): lax.all_to_all(cotan_all, 'dp', split_axis=1, concat_axis=0, tiled=True)  28.7 us
    reduce_scatter x1, waiting for transfers between devices, per_device(): lax.psum_scatter(lax.dot_general(pre_grad, up_weight, (((1,), (1,)), ((),...  18.9 us
    dynamic_update_slice x1, local copies, waits for them, and re-layouts, ring_gather(): lax.dynamic_update_slice_in_dim(result, shard, index * rows, axis=dim)  16.2 us
    dot_general x1, matrix products, per_device(): lax.dot_general(pre_grad, up_weight, (((1,), (1,)), ((), ())), preferred_...  14.4 us
    dot_general x1, matrix products, per_device(): lax.dot_general(cotan_all, down_weight, (((1,), (1,)), ((), ())), preferr...  14.3 us
  transfers between devices with their start and end apart: 12, of which 7 were waited for; matrix products, arithmetic and copies ran while one was open for 60% of the time, Pallas kernels for 0%

profile of v1, /device:TPU:10, one launch (start us, length us, event | category | flops | bytes accessed | tf_op | source)
XLA Modules:
  0.0 377.5 jit_solution(7640775667031258969)
XLA Ops:
  7.2 1.1 convert_reduce_fusion.2
  8.3 1.2 fusion.19
  9.5 1.1 fusion.13
  10.5 0.1 collective-permute-start
  10.7 1.8 collective-permute-start.1
  12.5 3.2 collective-permute-done
  15.7 1.9 collective-permute-done.1
  17.6 1.9 collective-permute-start.3
  19.5 1.3 collective-permute-done.2
  20.8 11.6 %collective-permute-done.3 = bf16[16,6144]{1,0:T(8,128)(2,1)S(1)} collective-permute-done((bf16[16,6144]{1,0:T(8,128)(2,1)S(1)}, bf16[16,6144]{1,0:T(8,128)(2,1)S(1)}, u32[]{:S(2)}, u32[]{:S(2)}) %collective-permute-start.3) | collective-permute-done | bytes 196640 | tf_op jit(solution)/shard_map/ppermute | solution.py:22
  32.4 4.2 %collective-permute-start.5 = (bf16[16,6144]{1,0:T(8,128)(2,1)S(1)}, bf16[16,6144]{1,0:T(8,128)(2,1)S(1)}, u32[]{:S(2)}, u32[]{:S(2)}) collective-permute-start(bf16[16,6144]{1,0:T(8,128)(2,1)S(1)} %collective-permute-done.3), channel_id=1, source_target_pairs={{0,7},{1,0},{2,1},{3,2},{4,3},{5,4},{6,5},{7,6},{8,15},{9,8},{10,9... | collective-permute-start | bytes 589832 | tf_op jit(solution)/shard_map/ppermute | solution.py:22
  36.6 0.8 copy.31
  37.4 1.3 broadcast_in_dim.2
  38.8 16.2 %dynamic_update_slice.24 = bf16[128,6144]{0,1:T(8,128)(2,1)} dynamic-update-slice(bf16[128,6144]{0,1:T(8,128)(2,1)} %broadcast_in_dim.2, bf16[16,6144]{0,1:T(8,128)(2,1)S(1)} %copy.31, s32[]{:T(128)S(6)} %select_n.55, s32[]{:T(128)} %constant.70.clone.1) | dynamic-update-slice | bytes 393220 | tf_op jit(solution)/shard_map/dynamic_update_slice | solution.py:13
  55.0 0.8 copy.32
  55.8 16.2 %dynamic_update_slice.25 = bf16[128,6144]{0,1:T(8,128)(2,1)} dynamic-update-slice(bf16[128,6144]{0,1:T(8,128)(2,1)} %dynamic_update_slice.24, bf16[16,6144]{0,1:T(8,128)(2,1)S(1)} %copy.32, s32[]{:T(128)S(6)} %select_n.57, s32[]{:T(128)} %constant.70.clone.1) | dynamic-update-slice | bytes 393220 | tf_op jit(solution)/shard_map/dynamic_update_slice | solution.py:18
  72.0 0.8 copy.33
  72.8 16.2 %dynamic_update_slice.26 = bf16[128,6144]{0,1:T(8,128)(2,1)} dynamic-update-slice(bf16[128,6144]{0,1:T(8,128)(2,1)} %dynamic_update_slice.25, bf16[16,6144]{0,1:T(8,128)(2,1)S(1)} %copy.33, s32[]{:T(128)S(6)} %select_n.59, s32[]{:T(128)} %constant.70.clone.1) | dynamic-update-slice | bytes 393220 | tf_op jit(solution)/shard_map/dynamic_update_slice | solution.py:23
  89.1 0.8 copy.34
  89.9 13.7 %dynamic_update_slice.27 = bf16[128,6144]{0,1:T(8,128)(2,1)} dynamic-update-slice(bf16[128,6144]{0,1:T(8,128)(2,1)} %dynamic_update_slice.26, bf16[16,6144]{0,1:T(8,128)(2,1)S(1)} %copy.34, s32[]{:T(128)S(6)} %select_n.61, s32[]{:T(128)} %constant.70.clone.1) | dynamic-update-slice | bytes 393220 | tf_op jit(solution)/shard_map/dynamic_update_slice | solution.py:18
  103.6 0.8 copy.35
  104.4 16.2 %dynamic_update_slice.28 = bf16[128,6144]{0,1:T(8,128)(2,1)} dynamic-update-slice(bf16[128,6144]{0,1:T(8,128)(2,1)} %dynamic_update_slice.27, bf16[16,6144]{0,1:T(8,128)(2,1)S(1)} %copy.35, s32[]{:T(128)S(6)} %select_n.63, s32[]{:T(128)} %constant.70.clone.1) | dynamic-update-slice | bytes 393220 | tf_op jit(solution)/shard_map/dynamic_update_slice | solution.py:23
  120.6 0.8 copy.36
  121.4 16.2 %dynamic_update_slice.29 = bf16[128,6144]{0,1:T(8,128)(2,1)} dynamic-update-slice(bf16[128,6144]{0,1:T(8,128)(2,1)} %dynamic_update_slice.28, bf16[16,6144]{0,1:T(8,128)(2,1)S(1)} %copy.36, s32[]{:T(128)S(6)} %select_n.65, s32[]{:T(128)} %constant.70.clone.1) | dynamic-update-slice | bytes 393220 | tf_op jit(solution)/shard_map/dynamic_update_slice | solution.py:18
  137.7 0.8 copy.37
  138.5 16.2 %dynamic_update_slice.30 = bf16[128,6144]{0,1:T(8,128)(2,1)} dynamic-update-slice(bf16[128,6144]{0,1:T(8,128)(2,1)} %dynamic_update_slice.29, bf16[16,6144]{0,1:T(8,128)(2,1)S(1)} %copy.37, s32[]{:T(128)S(6)} %select_n.67, s32[]{:T(128)} %constant.70.clone.1) | dynamic-update-slice | bytes 393220 | tf_op jit(solution)/shard_map/dynamic_update_slice | solution.py:23
  154.7 0.8 copy.38
  155.5 16.2 %dynamic_update_slice.31 = bf16[128,6144]{0,1:T(8,128)(2,1)} dynamic-update-slice(bf16[128,6144]{0,1:T(8,128)(2,1)} %dynamic_update_slice.30, bf16[16,6144]{0,1:T(8,128)(2,1)S(1)} %copy.38, s32[]{:T(128)S(6)} %select_n.69, s32[]{:T(128)} %constant.70.clone.1) | dynamic-update-slice | bytes 393220 | tf_op jit(solution)/shard_map/dynamic_update_slice | solution.py:18
  171.7 12.9 %multiply_convert_fusion.2 = (bf16[128,2048]{1,0:T(8,128)(2,1)}, f32[128,2048]{1,0:T(8,128)S(1)}) fusion(bf16[128,6144]{0,1:T(8,128)(2,1)} %dynamic_update_slice.31, bf16[6144,2048]{1,0:T(8,128)(2,1)} %param.7), kind=kOutput, calls=%fused_computation.15 | convolution fusion | flops 3222536192 | bytes 28311552 | tf_op jit(solution)/shard_map/dot_general | solution.py:50
  184.7 0.2 all-gather.6.cloned.1.call-start
  185.0 14.3 %fusion = bf16[128,2048]{1,0:T(8,128)(2,1)} fusion(bf16[128,6144]{1,0:T(8,128)(2,1)} %all-gather.4.cloned.1.call-done, bf16[2048,6144]{1,0:T(8,128)(2,1)} %param.8, f32[128,2048]{1,0:T(8,128)S(1)} %get-tuple-element.8), kind=kOutput, calls=%fused_computation.7 | convolution fusion | flops 3223846912 | bytes 28311552 | tf_op jit(solution)/shard_map/dot_general | solution.py:52
  199.3 14.4 %fusion.20 = f32[128,6144]{1,0:T(8,128)} fusion(bf16[128,2048]{1,0:T(8,128)(2,1)} %fusion, bf16[6144,2048]{1,0:T(8,128)(2,1)} %param.7), kind=kOutput, calls=%fused_computation.38 | convolution fusion | flops 3221225472 | bytes 28835840 | tf_op jit(solution)/shard_map/dot_general | solution.py:57
  213.8 1.4 copy-done
  215.1 0.9 copy.40
  216.0 0.7 copy.41
  216.8 28.7 %all_to_all.32 = bf16[128,4,1536]{2,0,1:T(8,128)(2,1)S(1)} all-to-all(bf16[128,4,1536]{2,0,1:T(8,128)(2,1)S(1)} %copy.41), channel_id=1, replica_groups=mesh['dp'=4,'mp'=8] {'dp'}, dimensions={1} | all-to-all | bytes 3145728 | tf_op jit(solution)/shard_map/all_to_all | solution.py:76
  245.5 4.1 %all-to-all-start = ((bf16[128,4,1536]{0,2,1:T(8,128)(2,1)}), bf16[128,4,1536]{0,2,1:T(8,128)(2,1)S(1)}, u32[]{:S(2)}, u32[]{:S(2)}) async-start(bf16[128,4,1536]{0,2,1:T(8,128)(2,1)} %bitcast), calls=%async_computation.1 | async-start | bytes 3145728 | tf_op jit(solution)/shard_map/all_to_all | solution.py:75
  249.6 14.2 %convert_reduce_fusion = f32[2048,1536]{1,0:T(8,128)} fusion(bf16[4,128,2048]{2,1,0:T(8,128)(2,1)} %bitcast.19, bf16[128,4,1536]{2,0,1:T(8,128)(2,1)S(1)} %all_to_all.32), kind=kOutput, calls=%fused_computation | convolution fusion | flops 3255828480 | bytes 16252928 | tf_op jit(solution)/shard_map/rtf,rtk->rfk/dot_general | solution.py:89
  263.8 9.0 %multiply_convert_fusion = bf16[2048,1536]{1,0:T(8,128)(2,1)} fusion(f32[2048,1536]{1,0:T(8,128)} %convert_reduce_fusion), kind=kLoop, calls=%fused_computation.4 | loop fusion | flops 6291456 | bytes 18874368 | tf_op jit(solution)/shard_map/convert_element_type | solution.py:95
  272.8 7.4 %all-to-all-done = bf16[128,4,1536]{0,2,1:T(8,128)(2,1)S(1)} async-done(((bf16[128,4,1536]{0,2,1:T(8,128)(2,1)}), bf16[128,4,1536]{0,2,1:T(8,128)(2,1)S(1)}, u32[]{:S(2)}, u32[]{:S(2)}) %all-to-all-start) | async-done | bytes 1572896 | tf_op jit(solution)/shard_map/all_to_all | solution.py:75
  280.2 0.2 all-gather.6.cloned.1.call-done
  280.4 14.1 %convert_reduce_fusion.1 = f32[1536,2048]{1,0:T(8,128)} fusion(bf16[4,128,2048]{2,1,0:T(8,128)(2,1)} %bitcast.20, bf16[128,4,1536]{0,2,1:T(8,128)(2,1)S(1)} %all-to-all-done), kind=kOutput, calls=%fused_computation.1 | convolution fusion | flops 3255828480 | bytes 16252928 | tf_op jit(solution)/shard_map/rtk,rtf->rkf/dot_general | solution.py:86
  294.5 9.3 %multiply_convert_fusion.1 = bf16[1536,2048]{1,0:T(8,128)(2,1)} fusion(f32[1536,2048]{1,0:T(8,128)} %convert_reduce_fusion.1), kind=kLoop, calls=%fused_computation.5 | loop fusion | flops 6291456 | bytes 18874368 | tf_op jit(solution)/shard_map/convert_element_type | solution.py:94
  303.7 18.9 %reduce-scatter.2.cloned.1.call-done = f32[16,6144]{1,0:T(8,128)} async-done(((f32[128,6144]{1,0:T(8,128)}), f32[16,6144]{1,0:T(8,128)}) %reduce-scatter.2.cloned.1.call-update) | async-done | bytes 393232 | tf_op jit(solution)/shard_map/reduce_scatter | solution.py:56
  322.6 1.3 fusion.18
  323.9 44.6 %psum.7 = f32[6144]{0:T(1024)S(1)} all-reduce(f32[6144]{0:T(1024)S(1)} %get-tuple-element.4), channel_id=1, replica_groups=mesh['dp'=4,'mp'=8] {'dp','mp'}, use_global_device_ids=true, to_apply=%region_8.9 | all-reduce | flops 6144 | bytes 49152 | tf_op jit(solution)/shard_map/psum | solution.py:67
  368.5 0.6 broadcast_multiply_fusion
  369.1 1.8 fusion.17
  (23 shorter events, 0.2 us)
Async XLA Ops:
  7.2 177.8 %all-gather.4.cloned.1.call-start = ((), (), s32[]{:S(2)}) async-start(), calls=%async_computation.3 | async-start | bytes 1769472 | tf_op jit(solution)/shard_map/all_gather | solution.py:48
  10.5 5.1 %collective-permute-start = (bf16[16,6144]{1,0:T(8,128)(2,1)S(1)}, bf16[16,6144]{1,0:T(8,128)(2,1)S(1)}, u32[]{:S(2)}, u32[]{:S(2)}) collective-permute-start(bf16[16,6144]{1,0:T(8,128)(2,1)S(1)} %fusion.13), channel_id=1, source_target_pairs={{0,1},{1,2},{2,3},{3,4},{4,5},{5,6},{6,7},{7,0},{8,9},{9,10},{10,1... | collective-permute-start | bytes 589832 | tf_op jit(solution)/shard_map/ppermute | solution.py:17
  10.6 239.0 %all-gather.8.cloned.1.call-start = ((), (), s32[]{:S(2)}) async-start(), calls=%async_computation.6 | async-start | bytes 2621440 | tf_op jit(solution)/shard_map/all_gather | solution.py:79
  10.7 6.9 %collective-permute-start.1 = (bf16[16,6144]{1,0:T(8,128)(2,1)S(1)}, bf16[16,6144]{1,0:T(8,128)(2,1)S(1)}, u32[]{:S(2)}, u32[]{:S(2)}) collective-permute-start(bf16[16,6144]{1,0:T(8,128)(2,1)S(1)} %fusion.13), channel_id=1, source_target_pairs={{0,7},{1,0},{2,1},{3,2},{4,3},{5,4},{6,5},{7,6},{8,15},{9,8},{10,9... | collective-permute-start | bytes 589832 | tf_op jit(solution)/shard_map/ppermute | solution.py:22
  15.7 5.1 %collective-permute-start.2 = (bf16[16,6144]{1,0:T(8,128)(2,1)S(1)}, bf16[16,6144]{1,0:T(8,128)(2,1)S(1)}, u32[]{:S(2)}, u32[]{:S(2)}) collective-permute-start(bf16[16,6144]{1,0:T(8,128)(2,1)S(1)} %collective-permute-done), channel_id=1, source_target_pairs={{0,1},{1,2},{2,3},{3,4},{4,5},{5,6},{6,7},{7,0},{8,9},{9,10},{10,1... | collective-permute-start | bytes 589832 | tf_op jit(solution)/shard_map/ppermute | solution.py:17
  17.6 14.8 %collective-permute-start.3 = (bf16[16,6144]{1,0:T(8,128)(2,1)S(1)}, bf16[16,6144]{1,0:T(8,128)(2,1)S(1)}, u32[]{:S(2)}, u32[]{:S(2)}) collective-permute-start(bf16[16,6144]{1,0:T(8,128)(2,1)S(1)} %collective-permute-done.1), channel_id=1, source_target_pairs={{0,7},{1,0},{2,1},{3,2},{4,3},{5,4},{6,5},{7,6},{8,15},{9,8},{10,9... | collective-permute-start | bytes 589832 | tf_op jit(solution)/shard_map/ppermute | solution.py:22
  20.8 15.8 %collective-permute-start.4 = (bf16[16,6144]{1,0:T(8,128)(2,1)S(1)}, bf16[16,6144]{1,0:T(8,128)(2,1)S(1)}, u32[]{:S(2)}, u32[]{:S(2)}) collective-permute-start(bf16[16,6144]{1,0:T(8,128)(2,1)S(1)} %collective-permute-done.2), channel_id=1, source_target_pairs={{0,1},{1,2},{2,3},{3,4},{4,5},{5,6},{6,7},{7,0},{8,9},{9,10},{10,1... | collective-permute-start | bytes 589832 | tf_op jit(solution)/shard_map/ppermute | solution.py:17
  32.4 105.3 %collective-permute-start.5 = (bf16[16,6144]{1,0:T(8,128)(2,1)S(1)}, bf16[16,6144]{1,0:T(8,128)(2,1)S(1)}, u32[]{:S(2)}, u32[]{:S(2)}) collective-permute-start(bf16[16,6144]{1,0:T(8,128)(2,1)S(1)} %collective-permute-done.3), channel_id=1, source_target_pairs={{0,7},{1,0},{2,1},{3,2},{4,3},{5,4},{6,5},{7,6},{8,15},{9,8},{10,9... | collective-permute-start | bytes 589832 | tf_op jit(solution)/shard_map/ppermute | solution.py:22
  36.6 118.1 %collective-permute-start.6 = (bf16[16,6144]{1,0:T(8,128)(2,1)S(1)}, bf16[16,6144]{1,0:T(8,128)(2,1)S(1)}, u32[]{:S(2)}, u32[]{:S(2)}) collective-permute-start(bf16[16,6144]{1,0:T(8,128)(2,1)S(1)} %collective-permute-done.4), channel_id=1, source_target_pairs={{0,1},{1,2},{2,3},{3,4},{4,5},{5,6},{6,7},{7,0},{8,9},{9,10},{10,1... | collective-permute-start | bytes 589832 | tf_op jit(solution)/shard_map/ppermute | solution.py:17
  184.7 95.7 %all-gather.6.cloned.1.call-start = ((), (), s32[]{:S(2)}) async-start(), calls=%async_computation.5 | async-start | bytes 2621440 | tf_op jit(solution)/shard_map/all_gather | solution.py:80
  199.3 123.4 %reduce-scatter.2.cloned.1.call-start = ((), (), s32[]{:S(2)}) async-start(), calls=%async_computation.4 | async-start | bytes 3538944 | tf_op jit(solution)/shard_map/reduce_scatter | solution.py:56
  213.7 1.4 copy-start
  245.5 34.7 %all-to-all-start = ((bf16[128,4,1536]{0,2,1:T(8,128)(2,1)}), bf16[128,4,1536]{0,2,1:T(8,128)(2,1)S(1)}, u32[]{:S(2)}, u32[]{:S(2)}) async-start(bf16[128,4,1536]{0,2,1:T(8,128)(2,1)} %bitcast), calls=%async_computation.1 | async-start | bytes 3145728 | tf_op jit(solution)/shard_map/all_to_all | solution.py:75
  294.4 28.2 %copy-start.1 = (bf16[16,6144]{1,0:T(8,128)(2,1)S(1)}, bf16[16,6144]{1,0:T(8,128)(2,1)}, u32[]{:S(2)}) copy-start(bf16[16,6144]{1,0:T(8,128)(2,1)} %param.5) | copy-start | bytes 589828
  294.4 28.2 %copy-start.2 = (f32[6144]{0:T(1024)S(1)}, f32[6144]{0:T(1024)}, u32[]{:S(2)}) copy-start(f32[6144]{0:T(1024)} %param.6) | copy-start | bytes 73732
Sparse Core Ops, SparseCore 0:
  10.8 32.6 all-gather.3
  184.8 44.2 all-gather.7
  231.0 49.3 all-gather.5
  282.5 40.0 reduce-scatter.1
